TPU v7x, 32 devices: a whole 2x2x4 slice. The times are simulated.
32 devices in a mesh: dp: 16 (over z, y, x), mp: 2 (over core).
Axes of the slice: x: 2, y: 2, z: 4, core: 2. Of those that a mesh axis runs over, the one named last changes fastest.
Arguments:
- tokens: bfloat16 [8192, 2048], P('dp'), may hold values from -6 to 6
- noise_cond: float32 [128, 8192], P('dp'), may hold values from -1.5 to 1.5
- slot_bucket: int32 [16], P('dp'), may hold values from 0 to 3, as said below
- image_height: int32 [16, 8], P('dp'), may hold values from 5 to 16, as said below
- image_width: int32 [16, 8], P('dp'), may hold values from 5 to 32, as said below
- weight_query: bfloat16 [2048, 2048], P('dp', 'mp'), may hold values from -0.1875 to 0.1875
- weight_key: bfloat16 [2048, 2048], P('dp', 'mp'), may hold values from -0.1875 to 0.1875
- weight_value: bfloat16 [2048, 2048], P('dp', 'mp'), may hold values from -0.125 to 0.125
- weight_out: bfloat16 [2048, 2048], P('mp', 'dp'), may hold values from -0.5 to 0.5
- weight_in: bfloat16 [2048, 8192], P('dp', 'mp'), may hold values from -0.125 to 0.125
- weight_back: bfloat16 [8192, 2048], P('mp', 'dp'), may hold values from -0.09375 to 0.09375
- cotangent: bfloat16 [8192, 2048], P('dp'), may hold values from -6 to 6
Outputs:
- block_output: bfloat16 [8192, 2048], P('dp')
- grad_tokens: float32 [8192, 2048], P('dp')
- grad_cond: float32 [128, 8192], P('dp')
- grad_query: float32 [2048, 2048], P('dp', 'mp')
- grad_key: float32 [2048, 2048], P('dp', 'mp')
- grad_value: float32 [2048, 2048], P('dp', 'mp')
- grad_out: float32 [2048, 2048], P('mp', 'dp')
- grad_in: float32 [2048, 8192], P('dp', 'mp')
- grad_back: float32 [8192, 2048], P('mp', 'dp')
Inputs may be any that keep to these rules, and one draw needn't show every extreme that they name: `slot_bucket`: buckets 0 to 3 hold 8, 4, 2, 1 images of a slot; the first slot is of bucket 3. `image_height`: greater than half of the bucket's grid height and at most it: 8 for buckets 0 and 1, 16 for buckets 2 and 3; entries of images past the slot's count are unused. `image_width`: greater than half of the bucket's grid width and at most it: 8, 16, 16, 32 for buckets 0 to 3; entries of images past the slot's count are unused.
All inputs are finite; a program needn't handle non-finite values.
Results may differ from a plain program's by a relative error of at most 0.014.
Values may be sent and summed in bfloat16 or wider, within the bound.
No kernel may reach another device: no remote copies, remote signals or barrier semaphores. Data moves between devices by JAX's collectives and lax.ppermute only.
A program may use at most 384 MiB of HBM per device.

v0:
```python
import jax
import jax.numpy as jnp
from jax import lax
from jax.sharding import Mesh, PartitionSpec as P

HD = 128
GW = 32
IMG_SLOT = 8
SLOT = 512
HALF = SLOT // 2
EPS = 1e-06
HIGH = lax.Precision.HIGHEST
BF = jnp.bfloat16
F32 = jnp.float32
PAIRED = (0, 4, 1, 6, 2, 5, 3, 7)
UNPAIRED = (0, 2, 4, 6, 1, 5, 3, 7)


def arrange(slot_bucket, image_height, image_width, places):
    choose = (slot_bucket[:, None] == jnp.arange(4, dtype=jnp.int32)[None, :]).astype(jnp.int32)
    areas = jnp.sum(
        choose * jnp.array([SLOT // 8, SLOT // 4, SLOT // 2, SLOT], jnp.int32)[None, :], axis=1
    )
    across = jnp.sum(
        choose * jnp.array([GW // 4, GW // 2, GW // 2, GW], jnp.int32)[None, :], axis=1
    )
    image = places[None, :] // areas[:, None]
    inner = places[None, :] % areas[:, None]
    grid_row = inner // across[:, None]
    grid_col = inner % across[:, None]
    member = image[:, :, None] == jnp.arange(IMG_SLOT, dtype=jnp.int32)[None, None, :]
    tall = jnp.sum(jnp.where(member, image_height[:, None, :], 0), axis=2)
    broad = jnp.sum(jnp.where(member, image_width[:, None, :], 0), axis=2)
    real = (grid_row < tall) & (grid_col < broad)
    return (image, real)


def modulate(hidden, member, cond_part):
    width = hidden.shape[-1]
    mods = jnp.einsum("ti,ic->tc", member, cond_part, precision=HIGH)
    factor = lax.rsqrt(jnp.mean(hidden * hidden, axis=-1, keepdims=True) + EPS)
    return hidden * factor * (1.0 + mods[:, :width]) + mods[:, width:]


def contract_rows(left, right):
    return lax.dot_general(left, right, (((0,), (0,)), ((), ())), preferred_element_type=F32)


def times_transposed(left, right):
    return lax.dot_general(left, right, (((1,), (1,)), ((), ())), preferred_element_type=F32)


def times(left, right):
    return jnp.dot(left, right, preferred_element_type=F32)


def reorder(rows, order):
    blocks = rows.reshape(8, HALF, rows.shape[-1])
    return jnp.concatenate([blocks[i] for i in order], axis=0)


def heads_of(rows):
    return rows.reshape(4, SLOT, -1, HD)


def attend_forward(queries, keys_low, values, allowed):
    scores = jnp.einsum("sqhd,skhd->shqk", queries, keys_low, preferred_element_type=F32) * HD ** (
        -0.5
    )
    scores = jnp.where(allowed, scores, -1e30)
    top = jnp.max(scores, axis=-1, keepdims=True)
    weights = jnp.where(allowed, jnp.exp(scores - top), 0.0)
    total = jnp.sum(weights, axis=-1, keepdims=True)
    probs = (weights / total).astype(BF)
    mixed = jnp.einsum("shqk,skhd->sqhd", probs, values, preferred_element_type=F32)
    return (mixed.astype(BF).reshape(4 * SLOT, -1), top + jnp.log(total))


def attend_backward(queries, keys_low, values, allowed, logsum, grad_mixed):
    scale = HD ** (-0.5)
    scores = jnp.einsum("sqhd,skhd->shqk", queries, keys_low, preferred_element_type=F32) * scale
    probs = jnp.where(allowed, jnp.exp(scores - logsum), 0.0)
    grad_values = jnp.einsum(
        "shqk,sqhd->skhd", probs.astype(BF), grad_mixed, preferred_element_type=F32
    )
    grad_probs = jnp.einsum("sqhd,skhd->shqk", grad_mixed, values, preferred_element_type=F32)
    grad_scores = probs * (grad_probs - jnp.sum(probs * grad_probs, axis=-1, keepdims=True))
    grad_scores = grad_scores.astype(BF)
    grad_queries = (
        jnp.einsum("shqk,skhd->sqhd", grad_scores, keys_low, preferred_element_type=F32) * scale
    )
    grad_keys = (
        jnp.einsum("shqk,sqhd->skhd", grad_scores, queries, preferred_element_type=F32) * scale
    )
    return tuple(
        (part.astype(BF).reshape(4 * SLOT, -1) for part in (grad_queries, grad_keys, grad_values))
    )


def solution(mesh):
    outer = mesh.shape["dp"] // 4
    inner_mesh = Mesh(mesh.devices.reshape(outer, 2, 2, 2), ("o", "y", "x", "mp"))
    every = ("o", "y", "x", "mp")

    def pairs(move):
        made = []
        for o in range(outer):
            for y in range(2):
                for x in range(2):
                    for m in range(2):
                        ty, tx, tm = move(y, x, m)
                        made.append(
                            (((o * 2 + y) * 2 + x) * 2 + m, ((o * 2 + ty) * 2 + tx) * 2 + tm)
                        )
        return made

    near = pairs(lambda y, x, m: (y, 1 - x, m) if m == 0 else (1 - y, x, m))
    next_near = pairs(lambda y, x, m: (1 - y, x, m) if m == 0 else (y, 1 - x, m))
    sibling = pairs(lambda y, x, m: (y, x, 1 - m))
    offsets = {k: pairs(lambda y, x, m, k=k: (y ^ k >> 1, x ^ k & 1, m)) for k in (1, 2, 3)}

    def move(value, how):
        return lax.ppermute(value, every, how)

    def gather_rows(own):
        first = jnp.concatenate([own, move(own, near)], axis=0)
        second = move(first, next_near)
        return jnp.concatenate([first, second, move(first, sibling), move(second, sibling)], axis=0)

    def scatter_rows(left, right):
        quarter = left.shape[0] // 4

        def part(i):
            return times_transposed(left[i * quarter : (i + 1) * quarter], right)

        far = part(1) + move(part(3).astype(BF), sibling).astype(F32)
        got = move(far.astype(BF), next_near)
        close = part(0) + move(part(2).astype(BF), sibling).astype(F32)
        close = close + got.astype(F32)
        return close[:HALF] + move(close[HALF:].astype(BF), near).astype(F32)

    def spread_weight(shard, blocks):
        rows = shard.shape[0]
        chip = lax.axis_index("y") * 2 + lax.axis_index("x")
        parts = shard.reshape(rows, blocks, 4, -1)
        width = parts.shape[-1]
        gathered = jnp.zeros((4, rows, blocks * width), shard.dtype)
        for k in range(4):
            there = chip ^ k
            piece = lax.dynamic_index_in_dim(parts, there, 2, keepdims=False)
            piece = piece.reshape(rows, blocks * width)
            if k:
                piece = move(piece, offsets[k])
            gathered = lax.dynamic_update_slice(gathered, piece[None], (there, 0, 0))
        gathered = gathered.reshape(4 * rows, blocks * width)
        return lax.all_gather(gathered, "o", axis=0, tiled=True)

    def collect_grad(partial, blocks):
        mine = lax.psum_scatter(partial, "o", scatter_dimension=0, tiled=True)
        chip = lax.axis_index("y") * 2 + lax.axis_index("x")
        rows = mine.shape[0] // 4
        width = mine.shape[1] // blocks
        mine = mine.reshape(4, rows, blocks, 1, width)
        result = jnp.zeros((rows, blocks, 4, width), F32)
        for k in range(4):
            there = chip ^ k
            piece = lax.dynamic_index_in_dim(mine, there, 0, keepdims=False)
            if k:
                piece = move(piece, offsets[k])
            result = lax.dynamic_update_slice(result, piece, (0, 0, there, 0))
        return result.reshape(rows, blocks, 4 * width)

    def local(
        tokens,
        noise_cond,
        slot_bucket,
        image_height,
        image_width,
        weight_query,
        weight_key,
        weight_value,
        weight_out,
        weight_in,
        weight_back,
        cotangent,
    ):
        core = lax.axis_index("mp")
        width = tokens.shape[1]
        places = (jnp.arange(SLOT, dtype=jnp.int32) + HALF * core) % SLOT
        facts = jnp.concatenate([slot_bucket[:, None], image_height, image_width], axis=1)
        facts = jnp.concatenate([facts, move(facts, near)], axis=0)
        facts = jnp.concatenate([facts, move(facts, next_near)], axis=0)
        image, real = arrange(
            facts[:, 0], facts[:, 1 : 1 + IMG_SLOT], facts[:, 1 + IMG_SLOT :], places
        )
        allowed = ((image[:, :, None] == image[:, None, :]) & real[:, None, :])[:, None]
        member = (image[0, :HALF, None] == jnp.arange(IMG_SLOT, dtype=jnp.int32)[None, :]).astype(
            F32
        )
        first_cond = noise_cond[:, : 2 * width]
        second_cond = noise_cond[:, 2 * width :]
        qkv_full = spread_weight(
            jnp.concatenate([weight_query, weight_key, weight_value], axis=1), 3
        )
        out_full = spread_weight(weight_out.T, 1)
        in_full = spread_weight(weight_in, 1)
        back_full = spread_weight(weight_back.T, 1)
        hidden = lax.dynamic_slice(tokens, (core * HALF, 0), (HALF, width)).astype(F32)
        grad_result = lax.dynamic_slice(cotangent, (core * HALF, 0), (HALF, width))
        first = gather_rows(modulate(hidden, member, first_cond).astype(BF))
        cotangents = gather_rows(grad_result)
        qkv = reorder(times(first, qkv_full).astype(BF), PAIRED)
        part = qkv.shape[1] // 3
        queries, keys_low, values = (heads_of(qkv[:, i * part : (i + 1) * part]) for i in range(3))
        attended, logsum = attend_forward(queries, keys_low, values, allowed)
        attended = reorder(attended, UNPAIRED)
        middle = hidden + scatter_rows(attended, out_full)
        second = gather_rows(modulate(middle, member, second_cond).astype(BF))
        before = times(second, in_full)

        def gelu_exact(pre_act):
            return jax.nn.gelu(pre_act, approximate=False)

        after, gelu_pullback = jax.vjp(gelu_exact, before)
        after = after.astype(BF)
        grad_back = collect_grad(contract_rows(cotangents, after), 1)
        grad_before = gelu_pullback(times(cotangents, back_full))[0].astype(BF)
        grad_in = collect_grad(contract_rows(second, grad_before), 1)
        grad_second = scatter_rows(grad_before, in_full)
        result = (middle + scatter_rows(after, back_full)).astype(BF)

        def norm(rows_in, cond_in):
            return modulate(rows_in, member, cond_in)

        unused, second_pullback = jax.vjp(norm, middle, second_cond)
        grad_middle_norm, grad_second_cond = second_pullback(grad_second)
        grad_middle = grad_result.astype(F32) + grad_middle_norm
        grad_branch = gather_rows(grad_middle.astype(BF))
        grad_out = collect_grad(contract_rows(grad_branch, attended), 1)
        grad_attended = reorder(times(grad_branch, out_full).astype(BF), PAIRED)
        grad_qkv = attend_backward(
            queries, keys_low, values, allowed, logsum, heads_of(grad_attended)
        )
        grad_qkv = reorder(jnp.concatenate(grad_qkv, axis=1), UNPAIRED)
        grad_qkv_weight = collect_grad(contract_rows(first, grad_qkv), 3)
        grad_first = scatter_rows(grad_qkv, qkv_full)
        unused, first_pullback = jax.vjp(norm, hidden, first_cond)
        grad_hidden_norm, grad_first_cond = first_pullback(grad_first)
        grad_tokens = grad_middle + grad_hidden_norm
        grad_cond = jnp.concatenate([grad_first_cond, grad_second_cond], axis=1)
        grad_cond = grad_cond + move(grad_cond, sibling)

        def both_halves(rows):
            other = move(rows, sibling)
            made = jnp.zeros((SLOT, width), rows.dtype)
            made = lax.dynamic_update_slice(made, rows, (core * HALF, 0))
            return lax.dynamic_update_slice(made, other, ((1 - core) * HALF, 0))

        return (
            both_halves(result),
            both_halves(grad_tokens),
            grad_cond,
            grad_qkv_weight[:, 0],
            grad_qkv_weight[:, 1],
            grad_qkv_weight[:, 2],
            grad_out[:, 0].T,
            grad_in[:, 0],
            grad_back[:, 0].T,
        )

    dp = ("o", "y", "x")
    return jax.shard_map(
        local,
        mesh=inner_mesh,
        in_specs=(
            P(dp, None),
            P(dp, None),
            P(dp),
            P(dp, None),
            P(dp, None),
            P(dp, "mp"),
            P(dp, "mp"),
            P(dp, "mp"),
            P("mp", dp),
            P(dp, "mp"),
            P("mp", dp),
            P(dp, None),
        ),
        out_specs=(
            P(dp, None),
            P(dp, None),
            P(dp, None),
            P(dp, "mp"),
            P(dp, "mp"),
            P(dp, "mp"),
            P("mp", dp),
            P(dp, "mp"),
            P("mp", dp),
        ),
        check_vma=False,
    )
```

profile of v0, /device:TPU:0, one launch (start us, length us, event | category | flops | bytes accessed | tf_op | source)
XLA Modules:
  0.0 1036.5 jit_solution(10898821490958238784)
XLA Ops:
  55.9 22.7 %collective-permute-done.3 = bf16[512,2048]{1,0:T(8,128)(2,1)} collective-permute-done((bf16[512,2048]{1,0:T(8,128)(2,1)}, bf16[512,2048]{1,0:T(8,128)(2,1)}, u32[]{:S(2)}, u32[]{:S(2)}) %collective-permute-start.3) | collective-permute-done | bytes 2097184 | tf_op jit(solution)/shard_map/ppermute | solution.py:123
  92.9 11.5 %all-gather.5.cloned.1.call-done = bf16[2048,768]{1,0:T(8,128)(2,1)} async-done(((bf16[512,768]{1,0:T(8,128)(2,1)}), bf16[2048,768]{1,0:T(8,128)(2,1)}) %all-gather.5.cloned.1.call-update) | async-done | bytes 3145744 | tf_op jit(solution)/shard_map/all_gather | solution.py:156
  104.4 10.0 convolution_convert_fusion
  160.3 20.7 %collective-permute-done.14 = bf16[512,2048]{1,0:T(8,128)(2,1)} collective-permute-done((bf16[512,2048]{1,0:T(8,128)(2,1)}, bf16[512,2048]{1,0:T(8,128)(2,1)}, u32[]{:S(2)}, u32[]{:S(2)}) %collective-permute-start.14) | collective-permute-done | bytes 2097184 | tf_op jit(solution)/shard_map/ppermute | solution.py:123
  189.9 9.6 collective-permute-done.15
  241.9 9.2 collective-permute-done.24
  262.2 14.2 %collective-permute-done.17 = bf16[512,2048]{1,0:T(8,128)(2,1)} collective-permute-done((bf16[512,2048]{1,0:T(8,128)(2,1)}, bf16[512,2048]{1,0:T(8,128)(2,1)}, u32[]{:S(2)}, u32[]{:S(2)}) %collective-permute-start.17) | collective-permute-done | bytes 2097184 | tf_op jit(solution)/shard_map/ppermute | solution.py:123
  299.9 14.9 %fusion.132 = f32[2048,1024]{1,0:T(8,128)} fusion(bf16[2048,2048]{1,0:T(8,128)(2,1)} %constant_dynamic-update-slice_fusion.5, bf16[2048,1024]{1,0:T(8,128)(2,1)} %all-gather.9.cloned.1.call-done), kind=kOutput, calls=%fused_computation.344 | convolution fusion | flops 8589934592 | bytes 20971520 | tf_op jit(solution)/shard_map/dot_general | solution.py:54
  314.9 25.5 %all-gather.11.cloned.1.call-done = bf16[2048,1024]{1,0:T(8,128)(2,1)} async-done(((bf16[512,1024]{1,0:T(8,128)(2,1)}), bf16[2048,1024]{1,0:T(8,128)(2,1)}) %all-gather.11.cloned.1.call-update) | async-done | bytes 4194320 | tf_op jit(solution)/shard_map/all_gather | solution.py:156
  340.3 32.3 %add_convert_fusion = (bf16[2048,1024]{1,0:T(8,128)(2,1)S(1)}, f32[2048,1024]{1,0:T(8,128)}) fusion(f32[2048,1024]{1,0:T(8,128)} %fusion.132, bf16[2048,2048]{1,0:T(8,128)(2,1)} %constant_dynamic-update-slice_fusion.10, bf16[2048,1024]{1,0:T(8,128)(2,1)} %all-gather.11.cloned.1.call-done), kind=kOutput, calls=%fused_computation.5 | convolution fusion | flops 8740929536 | bytes 33554432 | tf_op jit(solution)/shard_map/dot_general | solution.py:54
  376.4 10.2 multiply_convert_fusion.1
  416.1 11.6 %collective-permute-done.37 = bf16[512,2048]{1,0:T(8,128)(2,1)S(1)} collective-permute-done((bf16[512,2048]{1,0:T(8,128)(2,1)}, bf16[512,2048]{1,0:T(8,128)(2,1)S(1)}, u32[]{:S(2)}, u32[]{:S(2)}) %collective-permute-start.37) | collective-permute-done | bytes 2097184 | tf_op jit(solution)/shard_map/ppermute | solution.py:123
  432.9 28.5 %collective-permute-done.28 = bf16[512,2048]{1,0:T(8,128)(2,1)S(1)} collective-permute-done((bf16[512,2048]{1,0:T(8,128)(2,1)}, bf16[512,2048]{1,0:T(8,128)(2,1)S(1)}, u32[]{:S(2)}, u32[]{:S(2)}) %collective-permute-start.28) | collective-permute-done | bytes 2097184 | tf_op jit(solution)/shard_map/ppermute | solution.py:123
  466.7 10.7 %collective-permute-done.29 = bf16[256,2048]{1,0:T(8,128)(2,1)S(1)} collective-permute-done((bf16[256,2048]{1,0:T(8,128)(2,1)S(1)}, bf16[256,2048]{1,0:T(8,128)(2,1)S(1)}, u32[]{:S(2)}, u32[]{:S(2)}) %collective-permute-start.29) | collective-permute-done | bytes 1048608 | tf_op jit(solution)/shard_map/ppermute | solution.py:123
  482.2 13.3 %collective-permute-done.39 = bf16[256,2048]{1,0:T(8,128)(2,1)S(1)} collective-permute-done((bf16[256,2048]{1,0:T(8,128)(2,1)S(1)}, bf16[256,2048]{1,0:T(8,128)(2,1)S(1)}, u32[]{:S(2)}, u32[]{:S(2)}) %collective-permute-start.39) | collective-permute-done | bytes 1048608 | tf_op jit(solution)/shard_map/ppermute | solution.py:123
  497.4 24.4 %collective-permute-done.40 = bf16[512,2048]{1,0:T(8,128)(2,1)S(1)} collective-permute-done((bf16[512,2048]{1,0:T(8,128)(2,1)S(1)}, bf16[512,2048]{1,0:T(8,128)(2,1)S(1)}, u32[]{:S(2)}, u32[]{:S(2)}) %collective-permute-start.40) | collective-permute-done | bytes 2097184 | tf_op jit(solution)/shard_map/ppermute | solution.py:123
  535.1 14.7 %fusion.135 = f32[2048,1024]{1,0:T(8,128)} fusion(bf16[2048,2048]{1,0:T(8,128)(2,1)} %constant_dynamic-update-slice_fusion.5, bf16[2048,1024]{1,0:T(8,128)(2,1)} %copy-done.75), kind=kOutput, calls=%fused_computation.347 | convolution fusion | flops 8589934592 | bytes 20971520 | tf_op jit(solution)/shard_map/dot_general | solution.py:46
  549.9 14.7 %fusion.136 = f32[2048,1024]{1,0:T(8,128)} fusion(bf16[2048,2048]{1,0:T(8,128)(2,1)} %constant_dynamic-update-slice_fusion.10, bf16[2048,1024]{1,0:T(8,128)(2,1)} %multiply_convert_fusion.1), kind=kOutput, calls=%fused_computation.348 | convolution fusion | flops 8589934592 | bytes 20971520 | tf_op jit(solution)/shard_map/dot_general | solution.py:46
  609.6 9.1 fusion.133
  635.4 21.0 %collective-permute-done.45 = bf16[512,2048]{1,0:T(8,128)(2,1)} collective-permute-done((bf16[512,2048]{1,0:T(8,128)(2,1)}, bf16[512,2048]{1,0:T(8,128)(2,1)}, u32[]{:S(2)}, u32[]{:S(2)}) %collective-permute-start.45) | collective-permute-done | bytes 2097184 | tf_op jit(solution)/shard_map/ppermute | solution.py:123
  694.1 29.4 %reduce-scatter.9.cloned.1.call-done = f32[512,1024]{1,0:T(8,128)} async-done(((f32[2048,1024]{1,0:T(8,128)}), f32[512,1024]{1,0:T(8,128)}) %reduce-scatter.9.cloned.1.call-update) | async-done | bytes 2097168 | tf_op jit(solution)/shard_map/reduce_scatter | solution.py:159
  734.4 136.8 %reduce-scatter.11.cloned.1.call-done = f32[512,1024]{1,0:T(8,128)} async-done(((f32[2048,1024]{1,0:T(8,128)}), f32[512,1024]{1,0:T(8,128)}) %reduce-scatter.11.cloned.1.call-update) | async-done | bytes 2097168 | tf_op jit(solution)/shard_map/reduce_scatter | solution.py:159
  899.7 11.3 %collective-permute-done.57 = f32[128,1,1,1024]{3,0,2,1:T(8,128)} collective-permute-done((f32[128,1,1,1024]{3,0,2,1:T(8,128)}, f32[128,1,1,1024]{3,0,2,1:T(8,128)}, u32[]{:S(2)}, u32[]{:S(2)}) %collective-permute-start.57) | collective-permute-done | bytes 524320 | tf_op jit(solution)/shard_map/ppermute | solution.py:123
  925.9 59.0 %reduce-scatter.5.cloned.1.call-done = f32[512,768]{1,0:T(8,128)} async-done(((f32[2048,768]{1,0:T(8,128)}), f32[512,768]{1,0:T(8,128)}) %reduce-scatter.5.cloned.1.call-update) | async-done | bytes 1572880 | tf_op jit(solution)/shard_map/reduce_scatter | solution.py:159
  (524 shorter events, 454.0 us)
Async XLA Ops:
  7.2 97.2 %all-gather.5.cloned.1.call-start = ((), (), s32[]{:S(2)}) async-start(), calls=%async_computation.4 | async-start | bytes 3932160 | tf_op jit(solution)/shard_map/all_gather | solution.py:156
  40.4 96.1 %all-gather.7.cloned.1.call-start = ((), (), s32[]{:S(2)}) async-start(), calls=%async_computation.5 | async-start | bytes 1310720 | tf_op jit(solution)/shard_map/all_gather | solution.py:156
  82.0 218.0 %all-gather.9.cloned.1.call-start = ((), (), s32[]{:S(2)}) async-start(), calls=%async_computation.6 | async-start | bytes 5242880 | tf_op jit(solution)/shard_map/all_gather | solution.py:156
  159.5 180.9 %all-gather.11.cloned.1.call-start = ((), (), s32[]{:S(2)}) async-start(), calls=%async_computation.7 | async-start | bytes 5242880 | tf_op jit(solution)/shard_map/all_gather | solution.py:156
  202.4 35.3 %collective-permute-start.16 = (bf16[256,2048]{1,0:T(8,128)(2,1)S(1)}, bf16[256,2048]{1,0:T(8,128)(2,1)}, u32[]{:S(2)}, u32[]{:S(2)}) collective-permute-start(bf16[256,2048]{1,0:T(8,128)(2,1)S(1)} %get-tuple-element.29), channel_id=1, source_target_pairs={{0,2},{1,5},{2,0},{3,7},{4,6},{5,1},{6,4},{7,3},{8,10},{9,13},{10,... | collective-permute-start | bytes 3145736 | tf_op jit(solution)/shard_map/ppermute | solution.py:123
  212.4 49.3 %collective-permute-start.32 = (bf16[512,2048]{1,0:T(8,128)(2,1)}, bf16[512,2048]{1,0:T(8,128)(2,1)}, u32[]{:S(2)}, u32[]{:S(2)}) collective-permute-start(bf16[512,2048]{1,0:T(8,128)(2,1)} %pad_maximum_fusion.2), channel_id=1, source_target_pairs={{0,4},{1,3},{2,6},{3,1},{4,0},{5,7},{6,2},{7,5},{8,12},{9,11},{10,... | collective-permute-start | bytes 6291464 | tf_op jit(solution)/shard_map/ppermute | solution.py:123
  240.5 35.9 %collective-permute-start.17 = (bf16[512,2048]{1,0:T(8,128)(2,1)}, bf16[512,2048]{1,0:T(8,128)(2,1)}, u32[]{:S(2)}, u32[]{:S(2)}) collective-permute-start(bf16[512,2048]{1,0:T(8,128)(2,1)} %pad_maximum_fusion.1), channel_id=1, source_target_pairs={{0,4},{1,3},{2,6},{3,1},{4,0},{5,7},{6,2},{7,5},{8,12},{9,11},{10,... | collective-permute-start | bytes 6291464 | tf_op jit(solution)/shard_map/ppermute | solution.py:123
  254.5 411.0 %reduce-scatter.7.cloned.1.call-start = ((), (), s32[]{:S(2)}) async-start(), calls=%async_computation.9 | async-start | bytes 2621440 | tf_op jit(solution)/shard_map/reduce_scatter | solution.py:159
  254.6 34.0 %collective-permute-start.33 = (bf16[512,2048]{1,0:T(8,128)(2,1)}, bf16[512,2048]{1,0:T(8,128)(2,1)S(1)}, u32[]{:S(2)}, u32[]{:S(2)}) collective-permute-start(bf16[512,2048]{1,0:T(8,128)(2,1)} %pad_maximum_fusion.2), channel_id=1, source_target_pairs={{0,1},{1,0},{2,3},{3,2},{4,5},{5,4},{6,7},{7,6},{8,9},{9,8},{10,11... | collective-permute-start | bytes 6291464 | tf_op jit(solution)/shard_map/ppermute | solution.py:123
  261.8 35.3 %collective-permute-start.18 = (bf16[512,2048]{1,0:T(8,128)(2,1)}, bf16[512,2048]{1,0:T(8,128)(2,1)S(1)}, u32[]{:S(2)}, u32[]{:S(2)}) collective-permute-start(bf16[512,2048]{1,0:T(8,128)(2,1)} %pad_maximum_fusion.1), channel_id=1, source_target_pairs={{0,1},{1,0},{2,3},{3,2},{4,5},{5,4},{6,7},{7,6},{8,9},{9,8},{10,11... | collective-permute-start | bytes 6291464 | tf_op jit(solution)/shard_map/ppermute | solution.py:123
  411.0 50.4 %collective-permute-start.28 = (bf16[512,2048]{1,0:T(8,128)(2,1)}, bf16[512,2048]{1,0:T(8,128)(2,1)S(1)}, u32[]{:S(2)}, u32[]{:S(2)}) collective-permute-start(bf16[512,2048]{1,0:T(8,128)(2,1)} %add_convert_fusion.3), channel_id=1, source_target_pairs={{0,4},{1,3},{2,6},{3,1},{4,0},{5,7},{6,2},{7,5},{8,12},{9,11},{10,... | collective-permute-start | bytes 6291464 | tf_op jit(solution)/shard_map/ppermute | solution.py:123
  429.0 35.1 %collective-permute-start.38 = (bf16[256,2048]{1,0:T(8,128)(2,1)S(1)}, bf16[256,2048]{1,0:T(8,128)(2,1)S(1)}, u32[]{:S(2)}, u32[]{:S(2)}) collective-permute-start(bf16[256,2048]{1,0:T(8,128)(2,1)S(1)} %slice.470), channel_id=1, source_target_pairs={{0,2},{1,5},{2,0},{3,7},{4,6},{5,1},{6,4},{7,3},{8,10},{9,13},{10,... | collective-permute-start | bytes 3145736 | tf_op jit(solution)/shard_map/ppermute | solution.py:123
  535.1 188.5 %reduce-scatter.9.cloned.1.call-start = ((), (), s32[]{:S(2)}) async-start(), calls=%async_computation.10 | async-start | bytes 10485760 | tf_op jit(solution)/shard_map/reduce_scatter | solution.py:159
  549.8 321.4 %reduce-scatter.11.cloned.1.call-start = ((), (), s32[]{:S(2)}) async-start(), calls=%async_computation.11 | async-start | bytes 10485760 | tf_op jit(solution)/shard_map/reduce_scatter | solution.py:159
  564.6 420.3 %reduce-scatter.5.cloned.1.call-start = ((), (), s32[]{:S(2)}) async-start(), calls=%async_computation.8 | async-start | bytes 7864320 | tf_op jit(solution)/shard_map/reduce_scatter | solution.py:159
  631.5 39.3 %collective-permute-start.30 = (bf16[256,2048]{1,0:T(8,128)(2,1)}, bf16[256,2048]{1,0:T(8,128)(2,1)}, u32[]{:S(2)}, u32[]{:S(2)}) collective-permute-start(bf16[256,2048]{1,0:T(8,128)(2,1)} %get-tuple-element.55), channel_id=1, source_target_pairs={{0,1},{1,0},{2,3},{3,2},{4,5},{5,4},{6,7},{7,6},{8,9},{9,8},{10,11... | collective-permute-start | bytes 3145736 | tf_op jit(solution)/shard_map/ppermute | solution.py:123
  693.7 181.7 %collective-permute-start.48 = (f32[8,8192]{1,0:T(8,128)}, f32[8,8192]{1,0:T(8,128)}, u32[]{:S(2)}, u32[]{:S(2)}) collective-permute-start(f32[8,8192]{1,0:T(8,128)} %pad_maximum_fusion.5), channel_id=1, source_target_pairs={{0,1},{1,0},{2,3},{3,2},{4,5},{5,4},{6,7},{7,6},{8,9},{9,8},{10,11... | collective-permute-start | bytes 786440 | tf_op jit(solution)/shard_map/ppermute | solution.py:123
  726.6 150.3 %collective-permute-start.55 = (f32[128,1,1,1024]{3,0,2,1:T(8,128)}, f32[128,1,1,1024]{3,0,2,1:T(8,128)S(1)}, u32[]{:S(2)}, u32[]{:S(2)}) collective-permute-start(f32[128,1,1,1024]{3,0,2,1:T(8,128)} %get-tuple-element.52), channel_id=1, source_target_pairs={{0,2},{1,3},{2,0},{3,1},{4,6},{5,7},{6,4},{7,5},{8,10},{9,11},{10,... | collective-permute-start | bytes 1572872 | tf_op jit(solution)/shard_map/ppermute | solution.py:123
  728.1 149.4 %collective-permute-start.56 = (f32[128,1,1,1024]{3,0,2,1:T(8,128)}, f32[128,1,1,1024]{3,0,2,1:T(8,128)S(1)}, u32[]{:S(2)}, u32[]{:S(2)}) collective-permute-start(f32[128,1,1,1024]{3,0,2,1:T(8,128)} %get-tuple-element.51), channel_id=1, source_target_pairs={{0,4},{1,5},{2,6},{3,7},{4,0},{5,1},{6,2},{7,3},{8,12},{9,13},{10,... | collective-permute-start | bytes 1572872 | tf_op jit(solution)/shard_map/ppermute | solution.py:123
  734.4 263.1 %collective-permute-start.47 = (f32[256,2048]{1,0:T(8,128)}, f32[256,2048]{1,0:T(8,128)}, u32[]{:S(2)}, u32[]{:S(2)}) collective-permute-start(f32[256,2048]{1,0:T(8,128)} %get-tuple-element.18), channel_id=1, source_target_pairs={{0,1},{1,0},{2,3},{3,2},{4,5},{5,4},{6,7},{7,6},{8,9},{9,8},{10,11... | collective-permute-start | bytes 6291464 | tf_op jit(solution)/shard_map/ppermute | solution.py:123
  873.9 45.8 %collective-permute-start.58 = (f32[128,1,1,1024]{3,0,2,1:T(8,128)}, f32[128,1,1,1024]{3,0,2,1:T(8,128)}, u32[]{:S(2)}, u32[]{:S(2)}) collective-permute-start(f32[128,1,1,1024]{3,0,2,1:T(8,128)} %get-tuple-element.48), channel_id=1, source_target_pairs={{0,2},{1,3},{2,0},{3,1},{4,6},{5,7},{6,4},{7,5},{8,10},{9,11},{10,... | collective-permute-start | bytes 1572872 | tf_op jit(solution)/shard_map/ppermute | solution.py:123
  875.4 45.5 %collective-permute-start.59 = (f32[128,1,1,1024]{3,0,2,1:T(8,128)}, f32[128,1,1,1024]{3,0,2,1:T(8,128)}, u32[]{:S(2)}, u32[]{:S(2)}) collective-permute-start(f32[128,1,1,1024]{3,0,2,1:T(8,128)} %get-tuple-element.47), channel_id=1, source_target_pairs={{0,4},{1,5},{2,6},{3,7},{4,0},{5,1},{6,2},{7,3},{8,12},{9,13},{10,... | collective-permute-start | bytes 1572872 | tf_op jit(solution)/shard_map/ppermute | solution.py:123
  876.9 45.3 %collective-permute-start.60 = (f32[128,1,1,1024]{3,0,2,1:T(8,128)}, f32[128,1,1,1024]{3,0,2,1:T(8,128)}, u32[]{:S(2)}, u32[]{:S(2)}) collective-permute-start(f32[128,1,1,1024]{3,0,2,1:T(8,128)} %get-tuple-element.46), channel_id=1, source_target_pairs={{0,6},{1,7},{2,4},{3,5},{4,2},{5,3},{6,0},{7,1},{8,14},{9,15},{10,... | collective-permute-start | bytes 1572872 | tf_op jit(solution)/shard_map/ppermute | solution.py:123
  877.4 33.6 %collective-permute-start.57 = (f32[128,1,1,1024]{3,0,2,1:T(8,128)}, f32[128,1,1,1024]{3,0,2,1:T(8,128)}, u32[]{:S(2)}, u32[]{:S(2)}) collective-permute-start(f32[128,1,1,1024]{3,0,2,1:T(8,128)} %get-tuple-element.50), channel_id=1, source_target_pairs={{0,6},{1,7},{2,4},{3,5},{4,2},{5,3},{6,0},{7,1},{8,14},{9,15},{10,... | collective-permute-start | bytes 1572872 | tf_op jit(solution)/shard_map/ppermute | solution.py:123
  (124 other events, 1884.1 us)
Sparse Core Ops, SparseCore 0:
  40.5 63.8 all-gather.4
  106.5 26.6 all-gather.6
  159.6 78.4 all-gather.8
  254.6 85.6 all-gather.10
  535.2 42.2 reduce-scatter.6
  579.7 143.8 reduce-scatter.8
  725.9 145.2 reduce-scatter.10
  873.5 111.3 reduce-scatter.4
where the time goes:
time: 1040 us
  waiting for transfers between devices  501 us (48%)
  local copies, waits for them, and re-layouts  197 us (19%)
  matrix products  196 us (19%)
  starting transfers between devices  70.7 us (7%)
  other arithmetic  55.2 us (5%)
  between operations  17.1 us (2%)
    ppermute x61, waiting for transfers between devices, move(): return lax.ppermute(value, every, how)  239 us
    reduce_scatter x4, waiting for transfers between devices, collect_grad(): mine = lax.psum_scatter(partial, 'o', scatter_dimension=0, tiled=True)  225 us
    ppermute x61, starting transfers between devices, move(): return lax.ppermute(value, every, how)  70.2 us
    dot_general x4, matrix products, times(): return jnp.dot(left, right, preferred_element_type=F32)  63 us
    unnamed x214, local copies, waits for them, and re-layouts  57.5 us
    dot_general x16, matrix products, times_transposed(): lax.dot_general(left, right, (((1,), (1,)), ((), ())), preferred_element_...  56.4 us
    dynamic_update_slice x16, local copies, waits for them, and re-layouts, collect_grad(): result = lax.dynamic_update_slice(result, piece, (0, 0, there, 0))  46.2 us
    dot_general x4, matrix products, contract_rows(): lax.dot_general(left, right, (((0,), (0,)), ((), ())), preferred_element_...  45.7 us
  transfers between devices with their start and end apart: 69, of which 25 were waited for; matrix products, arithmetic and copies ran while one was open for 36% of the time, Pallas kernels for 0%

commit v1 on v0

--- a/solution.py
+++ b/solution.py
@@ -153,7 +153,9 @@
                 piece = move(piece, offsets[k])
             gathered = lax.dynamic_update_slice(gathered, piece[None], (there, 0, 0))
         gathered = gathered.reshape(4 * rows, blocks * width)
-        return lax.all_gather(gathered, "o", axis=0, tiled=True)
+        return jnp.concatenate(
+            lax.all_to_all(jnp.stack([gathered] * lax.axis_size("o")), "o", 0, 0), axis=0
+        )
 
     def collect_grad(partial, blocks):
         mine = lax.psum_scatter(partial, "o", scatter_dimension=0, tiled=True)

time: 1040 us -> 1100 us (1.058)
  waiting for transfers between devices: 501 us -> 524 us
  matrix products: 196 us -> 215 us
    all_to_all x0 -> x4, waiting for transfers between devices: none -> 86.4 us  [spread_weight(): lax.all_to_all(jnp.stack([gathered] * lax.axis_size('o')), 'o', 0, 0)]
    all_gather x4 -> x0, waiting for transfers between devices: 37 us -> none  [spread_weight(): return lax.all_gather(gathered, 'o', axis=0, tiled=True)]
    reduce_scatter x4, waiting for transfers between devices: 225 us -> 205 us  [collect_grad(): mine = lax.psum_scatter(partial, 'o', scatter_dimension=0, tiled=True)]
    all_to_all x0 -> x4, starting transfers between devices: none -> 18.7 us  [spread_weight(): lax.all_to_all(jnp.stack([gathered] * lax.axis_size('o')), 'o', 0, 0)]
    dot_general x16, matrix products: 56.4 us -> 70.1 us  [times_transposed(): lax.dot_general(left, right, (((1,), (1,)), ((), ())), preferred_element_...]
    ppermute x61, starting transfers between devices: 70.2 us -> 58.4 us  [move(): return lax.ppermute(value, every, how)]
    unnamed x214 -> x210, local copies, waits for them, and re-layouts: 57.5 us -> 55.1 us
  transfers between devices with their start and end apart: 69 -> 69, of which waited for: 25 -> 26; matrix products, arithmetic and copies ran while one was open for 36% -> 36% of each run, Pallas kernels for 0% -> 0%
where the time goes in v1:
time: 1100 us; the launch traced here: 1090 us
  waiting for transfers between devices  524 us (48%)
  matrix products  215 us (20%)
  local copies, waits for them, and re-layouts  207 us (19%)
  starting transfers between devices  77.4 us (7%)
  other arithmetic  54.8 us (5%)
  between operations  16.7 us (2%)
    ppermute x61, waiting for transfers between devices, move(): return lax.ppermute(value, every, how)  232 us
    reduce_scatter x4, waiting for transfers between devices, collect_grad(): mine = lax.psum_scatter(partial, 'o', scatter_dimension=0, tiled=True)  205 us
    all_to_all x4, waiting for transfers between devices, spread_weight(): lax.all_to_all(jnp.stack([gathered] * lax.axis_size('o')), 'o', 0, 0)  86.4 us
    dot_general x16, matrix products, times_transposed(): lax.dot_general(left, right, (((1,), (1,)), ((), ())), preferred_element_...  70.1 us
    dot_general x4, matrix products, times(): return jnp.dot(left, right, preferred_element_type=F32)  62.9 us
    ppermute x61, starting transfers between devices, move(): return lax.ppermute(value, every, how)  58.4 us
    unnamed x210, local copies, waits for them, and re-layouts  55.1 us
    dot_general x4, matrix products, contract_rows(): lax.dot_general(left, right, (((0,), (0,)), ((), ())), preferred_element_...  45.7 us
  transfers between devices with their start and end apart: 69, of which 26 were waited for; matrix products, arithmetic and copies ran while one was open for 36% of the time, Pallas kernels for 0%

profile of v1, /device:TPU:0, one launch (start us, length us, event | category | flops | bytes accessed | tf_op | source)
XLA Modules:
  0.0 1094.3 jit_solution(5590488849405101510)
XLA Ops:
  37.3 10.6 collective-permute-done.6
  66.0 22.7 %collective-permute-done.3 = bf16[512,2048]{1,0:T(8,128)(2,1)} collective-permute-done((bf16[512,2048]{1,0:T(8,128)(2,1)}, bf16[512,2048]{1,0:T(8,128)(2,1)}, u32[]{:S(2)}, u32[]{:S(2)}) %collective-permute-start.3) | collective-permute-done | bytes 2097184 | tf_op jit(solution)/shard_map/ppermute | solution.py:123
  98.0 27.5 %all-to-all-done = bf16[4,512,768]{2,1,0:T(8,128)(2,1)} async-done(((bf16[4,512,768]{2,1,0:T(8,128)(2,1)}), bf16[4,512,768]{2,1,0:T(8,128)(2,1)}, u32[]{:S(2)}, u32[]{:S(2)}) %all-to-all-start) | async-done | bytes 3145760 | tf_op jit(solution)/shard_map/all_to_all | solution.py:157
  130.2 10.0 convolution_convert_fusion
  205.2 11.1 %collective-permute-done.14 = bf16[512,2048]{1,0:T(8,128)(2,1)} collective-permute-done((bf16[512,2048]{1,0:T(8,128)(2,1)S(1)}, bf16[512,2048]{1,0:T(8,128)(2,1)}, u32[]{:S(2)}, u32[]{:S(2)}) %collective-permute-start.14) | collective-permute-done | bytes 2097184 | tf_op jit(solution)/shard_map/ppermute | solution.py:123
  225.2 9.6 collective-permute-done.15
  255.2 15.7 %collective-permute-done.23 = bf16[128,1024]{1,0:T(8,128)(2,1)} collective-permute-done((bf16[128,1024]{1,0:T(8,128)(2,1)}, bf16[128,1024]{1,0:T(8,128)(2,1)}, u32[]{:S(2)}, u32[]{:S(2)}) %collective-permute-start.23) | collective-permute-done | bytes 262176 | tf_op jit(solution)/shard_map/ppermute | solution.py:123
  274.5 12.4 %collective-permute-done.24 = bf16[128,1024]{1,0:T(8,128)(2,1)} collective-permute-done((bf16[128,1024]{1,0:T(8,128)(2,1)}, bf16[128,1024]{1,0:T(8,128)(2,1)}, u32[]{:S(2)}, u32[]{:S(2)}) %collective-permute-start.24) | collective-permute-done | bytes 262176 | tf_op jit(solution)/shard_map/ppermute | solution.py:123
  330.7 14.8 %fusion.141 = f32[2048,1024]{1,0:T(8,128)} fusion(bf16[2048,2048]{1,0:T(8,128)(2,1)} %constant_dynamic-update-slice_fusion.5, bf16[2048,1024]{1,0:T(8,128)(2,1)} %bitcast.42), kind=kOutput, calls=%fused_computation.347 | convolution fusion | flops 8589934592 | bytes 20971520 | tf_op jit(solution)/shard_map/dot_general | solution.py:54
  345.6 51.2 %all-to-all-done.3 = bf16[4,512,1024]{2,1,0:T(8,128)(2,1)} async-done(((bf16[4,512,1024]{2,1,0:T(8,128)(2,1)}), bf16[4,512,1024]{2,1,0:T(8,128)(2,1)}, u32[]{:S(2)}, u32[]{:S(2)}) %all-to-all-start.3) | async-done | bytes 4194336 | tf_op jit(solution)/shard_map/all_to_all | solution.py:157
  396.8 32.2 %add_convert_fusion = (bf16[2048,1024]{1,0:T(8,128)(2,1)S(1)}, f32[2048,1024]{1,0:T(8,128)}) fusion(f32[2048,1024]{1,0:T(8,128)} %fusion.141, bf16[2048,2048]{1,0:T(8,128)(2,1)} %constant_dynamic-update-slice_fusion.10, bf16[2048,1024]{1,0:T(8,128)(2,1)} %bitcast.54), kind=kOutput, calls=%fused_computation.5 | convolution fusion | flops 8740929536 | bytes 33554432 | tf_op jit(solution)/shard_map/dot_general | solution.py:54
  493.1 27.2 %collective-permute-done.28 = bf16[512,2048]{1,0:T(8,128)(2,1)S(1)} collective-permute-done((bf16[512,2048]{1,0:T(8,128)(2,1)}, bf16[512,2048]{1,0:T(8,128)(2,1)S(1)}, u32[]{:S(2)}, u32[]{:S(2)}) %collective-permute-start.28) | collective-permute-done | bytes 2097184 | tf_op jit(solution)/shard_map/ppermute | solution.py:123
  524.9 11.6 %collective-permute-done.29 = bf16[256,2048]{1,0:T(8,128)(2,1)S(1)} collective-permute-done((bf16[256,2048]{1,0:T(8,128)(2,1)S(1)}, bf16[256,2048]{1,0:T(8,128)(2,1)S(1)}, u32[]{:S(2)}, u32[]{:S(2)}) %collective-permute-start.29) | collective-permute-done | bytes 1048608 | tf_op jit(solution)/shard_map/ppermute | solution.py:123
  540.4 14.2 %collective-permute-done.39 = bf16[256,2048]{1,0:T(8,128)(2,1)S(1)} collective-permute-done((bf16[256,2048]{1,0:T(8,128)(2,1)S(1)}, bf16[256,2048]{1,0:T(8,128)(2,1)S(1)}, u32[]{:S(2)}, u32[]{:S(2)}) %collective-permute-start.39) | collective-permute-done | bytes 1048608 | tf_op jit(solution)/shard_map/ppermute | solution.py:123
  556.6 24.3 %collective-permute-done.40 = bf16[512,2048]{1,0:T(8,128)(2,1)S(1)} collective-permute-done((bf16[512,2048]{1,0:T(8,128)(2,1)S(1)}, bf16[512,2048]{1,0:T(8,128)(2,1)S(1)}, u32[]{:S(2)}, u32[]{:S(2)}) %collective-permute-start.40) | collective-permute-done | bytes 2097184 | tf_op jit(solution)/shard_map/ppermute | solution.py:123
  594.0 14.6 %fusion.144 = f32[2048,1024]{1,0:T(8,128)} fusion(bf16[2048,2048]{1,0:T(8,128)(2,1)} %constant_dynamic-update-slice_fusion.5, bf16[2048,1024]{1,0:T(8,128)(2,1)} %copy-done.73), kind=kOutput, calls=%fused_computation.350 | convolution fusion | flops 8589934592 | bytes 20971520 | tf_op jit(solution)/shard_map/dot_general | solution.py:46
  608.6 14.6 %fusion.145 = f32[2048,1024]{1,0:T(8,128)} fusion(bf16[2048,2048]{1,0:T(8,128)(2,1)} %constant_dynamic-update-slice_fusion.10, bf16[2048,1024]{1,0:T(8,128)(2,1)} %copy-done.28), kind=kOutput, calls=%fused_computation.351 | convolution fusion | flops 8589934592 | bytes 20971520 | tf_op jit(solution)/shard_map/dot_general | solution.py:46
  687.0 9.3 fusion.142
  716.5 21.4 %collective-permute-done.45 = bf16[512,2048]{1,0:T(8,128)(2,1)} collective-permute-done((bf16[512,2048]{1,0:T(8,128)(2,1)}, bf16[512,2048]{1,0:T(8,128)(2,1)}, u32[]{:S(2)}, u32[]{:S(2)}) %collective-permute-start.45) | collective-permute-done | bytes 2097184 | tf_op jit(solution)/shard_map/ppermute | solution.py:123
  753.7 10.1 collective-permute-done.52
  772.2 9.7 reduce-scatter.9.cloned.1.call-done
  792.6 136.9 %reduce-scatter.11.cloned.1.call-done = f32[512,1024]{1,0:T(8,128)} async-done(((f32[2048,1024]{1,0:T(8,128)}), f32[512,1024]{1,0:T(8,128)}) %reduce-scatter.11.cloned.1.call-update) | async-done | bytes 2097168 | tf_op jit(solution)/shard_map/reduce_scatter | solution.py:161
  958.0 11.3 %collective-permute-done.57 = f32[128,1,1,1024]{3,0,2,1:T(8,128)} collective-permute-done((f32[128,1,1,1024]{3,0,2,1:T(8,128)}, f32[128,1,1,1024]{3,0,2,1:T(8,128)}, u32[]{:S(2)}, u32[]{:S(2)}) %collective-permute-start.57) | collective-permute-done | bytes 524320 | tf_op jit(solution)/shard_map/ppermute | solution.py:123
  984.2 58.9 %reduce-scatter.5.cloned.1.call-done = f32[512,768]{1,0:T(8,128)} async-done(((f32[2048,768]{1,0:T(8,128)}), f32[512,768]{1,0:T(8,128)}) %reduce-scatter.5.cloned.1.call-update) | async-done | bytes 1572880 | tf_op jit(solution)/shard_map/reduce_scatter | solution.py:161
  (519 shorter events, 495.5 us)
Async XLA Ops:
  54.5 70.9 %all-to-all-start = ((bf16[4,512,768]{2,1,0:T(8,128)(2,1)}), bf16[4,512,768]{2,1,0:T(8,128)(2,1)}, u32[]{:S(2)}, u32[]{:S(2)}) async-start(bf16[4,512,768]{2,1,0:T(8,128)(2,1)} %stack.12), calls=%async_computation | async-start | bytes 6291456 | tf_op jit(solution)/shard_map/all_to_all | solution.py:157
  126.5 41.6 %all-to-all-start.1 = ((bf16[4,512,256]{2,1,0:T(8,128)(2,1)}), bf16[4,512,256]{2,1,0:T(8,128)(2,1)S(1)}, u32[]{:S(2)}, u32[]{:S(2)}) async-start(bf16[4,512,256]{2,1,0:T(8,128)(2,1)} %stack.13), calls=%async_computation.1 | async-start | bytes 2097152 | tf_op jit(solution)/shard_map/all_to_all | solution.py:157
  198.5 98.1 %all-to-all-start.2 = ((bf16[4,512,1024]{2,1,0:T(8,128)(2,1)}), bf16[4,512,1024]{2,1,0:T(8,128)(2,1)}, u32[]{:S(2)}, u32[]{:S(2)}) async-start(bf16[4,512,1024]{2,1,0:T(8,128)(2,1)} %stack.14), calls=%async_computation.2 | async-start | bytes 8388608 | tf_op jit(solution)/shard_map/all_to_all | solution.py:157
  237.3 34.6 %collective-permute-start.16 = (bf16[256,2048]{1,0:T(8,128)(2,1)S(1)}, bf16[256,2048]{1,0:T(8,128)(2,1)S(1)}, u32[]{:S(2)}, u32[]{:S(2)}) collective-permute-start(bf16[256,2048]{1,0:T(8,128)(2,1)S(1)} %get-tuple-element.29), channel_id=1, source_target_pairs={{0,2},{1,5},{2,0},{3,7},{4,6},{5,1},{6,4},{7,3},{8,10},{9,13},{10,... | collective-permute-start | bytes 3145736 | tf_op jit(solution)/shard_map/ppermute | solution.py:123
  247.7 56.5 %collective-permute-start.32 = (bf16[512,2048]{1,0:T(8,128)(2,1)}, bf16[512,2048]{1,0:T(8,128)(2,1)}, u32[]{:S(2)}, u32[]{:S(2)}) collective-permute-start(bf16[512,2048]{1,0:T(8,128)(2,1)} %pad_maximum_fusion.2), channel_id=1, source_target_pairs={{0,4},{1,3},{2,6},{3,1},{4,0},{5,7},{6,2},{7,5},{8,12},{9,11},{10,... | collective-permute-start | bytes 6291464 | tf_op jit(solution)/shard_map/ppermute | solution.py:123
  252.0 34.9 %collective-permute-start.24 = (bf16[128,1024]{1,0:T(8,128)(2,1)}, bf16[128,1024]{1,0:T(8,128)(2,1)}, u32[]{:S(2)}, u32[]{:S(2)}) collective-permute-start(bf16[128,1024]{1,0:T(8,128)(2,1)} %bitcast.49), channel_id=1, source_target_pairs={{0,4},{1,5},{2,6},{3,7},{4,0},{5,1},{6,2},{7,3},{8,12},{9,13},{10,... | collective-permute-start | bytes 786440 | tf_op jit(solution)/shard_map/ppermute | solution.py:123
  253.8 34.2 %collective-permute-start.25 = (bf16[128,1024]{1,0:T(8,128)(2,1)}, bf16[128,1024]{1,0:T(8,128)(2,1)}, u32[]{:S(2)}, u32[]{:S(2)}) collective-permute-start(bf16[128,1024]{1,0:T(8,128)(2,1)} %bitcast.51), channel_id=1, source_target_pairs={{0,6},{1,7},{2,4},{3,5},{4,2},{5,3},{6,0},{7,1},{8,14},{9,15},{10,... | collective-permute-start | bytes 786440 | tf_op jit(solution)/shard_map/ppermute | solution.py:123
  273.4 38.8 %collective-permute-start.17 = (bf16[512,2048]{1,0:T(8,128)(2,1)}, bf16[512,2048]{1,0:T(8,128)(2,1)}, u32[]{:S(2)}, u32[]{:S(2)}) collective-permute-start(bf16[512,2048]{1,0:T(8,128)(2,1)} %pad_maximum_fusion.1), channel_id=1, source_target_pairs={{0,4},{1,3},{2,6},{3,1},{4,0},{5,7},{6,2},{7,5},{8,12},{9,11},{10,... | collective-permute-start | bytes 6291464 | tf_op jit(solution)/shard_map/ppermute | solution.py:123
  299.1 97.7 %all-to-all-start.3 = ((bf16[4,512,1024]{2,1,0:T(8,128)(2,1)}), bf16[4,512,1024]{2,1,0:T(8,128)(2,1)}, u32[]{:S(2)}, u32[]{:S(2)}) async-start(bf16[4,512,1024]{2,1,0:T(8,128)(2,1)} %stack.15), calls=%async_computation.3 | async-start | bytes 8388608 | tf_op jit(solution)/shard_map/all_to_all | solution.py:157
  304.1 442.4 %reduce-scatter.7.cloned.1.call-start = ((), (), s32[]{:S(2)}) async-start(), calls=%async_computation.9 | async-start | bytes 2621440 | tf_op jit(solution)/shard_map/reduce_scatter | solution.py:161
  472.5 47.8 %collective-permute-start.28 = (bf16[512,2048]{1,0:T(8,128)(2,1)}, bf16[512,2048]{1,0:T(8,128)(2,1)S(1)}, u32[]{:S(2)}, u32[]{:S(2)}) collective-permute-start(bf16[512,2048]{1,0:T(8,128)(2,1)} %add_convert_fusion.3), channel_id=1, source_target_pairs={{0,4},{1,3},{2,6},{3,1},{4,0},{5,7},{6,2},{7,5},{8,12},{9,11},{10,... | collective-permute-start | bytes 6291464 | tf_op jit(solution)/shard_map/ppermute | solution.py:123
  487.9 34.3 %collective-permute-start.38 = (bf16[256,2048]{1,0:T(8,128)(2,1)S(1)}, bf16[256,2048]{1,0:T(8,128)(2,1)S(1)}, u32[]{:S(2)}, u32[]{:S(2)}) collective-permute-start(bf16[256,2048]{1,0:T(8,128)(2,1)S(1)} %slice.474), channel_id=1, source_target_pairs={{0,2},{1,5},{2,0},{3,7},{4,6},{5,1},{6,4},{7,3},{8,10},{9,13},{10,... | collective-permute-start | bytes 3145736 | tf_op jit(solution)/shard_map/ppermute | solution.py:123
  593.9 188.0 %reduce-scatter.9.cloned.1.call-start = ((), (), s32[]{:S(2)}) async-start(), calls=%async_computation.10 | async-start | bytes 10485760 | tf_op jit(solution)/shard_map/reduce_scatter | solution.py:161
  608.6 320.9 %reduce-scatter.11.cloned.1.call-start = ((), (), s32[]{:S(2)}) async-start(), calls=%async_computation.11 | async-start | bytes 10485760 | tf_op jit(solution)/shard_map/reduce_scatter | solution.py:161
  623.3 419.8 %reduce-scatter.5.cloned.1.call-start = ((), (), s32[]{:S(2)}) async-start(), calls=%async_computation.8 | async-start | bytes 7864320 | tf_op jit(solution)/shard_map/reduce_scatter | solution.py:161
  712.7 38.5 %collective-permute-start.30 = (bf16[256,2048]{1,0:T(8,128)(2,1)}, bf16[256,2048]{1,0:T(8,128)(2,1)}, u32[]{:S(2)}, u32[]{:S(2)}) collective-permute-start(bf16[256,2048]{1,0:T(8,128)(2,1)} %get-tuple-element.55), channel_id=1, source_target_pairs={{0,1},{1,0},{2,3},{3,2},{4,5},{5,4},{6,7},{7,6},{8,9},{9,8},{10,11... | collective-permute-start | bytes 3145736 | tf_op jit(solution)/shard_map/ppermute | solution.py:123
  771.7 162.0 %collective-permute-start.48 = (f32[8,8192]{1,0:T(8,128)}, f32[8,8192]{1,0:T(8,128)}, u32[]{:S(2)}, u32[]{:S(2)}) collective-permute-start(f32[8,8192]{1,0:T(8,128)} %pad_maximum_fusion.5), channel_id=1, source_target_pairs={{0,1},{1,0},{2,3},{3,2},{4,5},{5,4},{6,7},{7,6},{8,9},{9,8},{10,11... | collective-permute-start | bytes 786440 | tf_op jit(solution)/shard_map/ppermute | solution.py:123
  784.9 150.2 %collective-permute-start.55 = (f32[128,1,1,1024]{3,0,2,1:T(8,128)}, f32[128,1,1,1024]{3,0,2,1:T(8,128)S(1)}, u32[]{:S(2)}, u32[]{:S(2)}) collective-permute-start(f32[128,1,1,1024]{3,0,2,1:T(8,128)} %get-tuple-element.52), channel_id=1, source_target_pairs={{0,2},{1,3},{2,0},{3,1},{4,6},{5,7},{6,4},{7,5},{8,10},{9,11},{10,... | collective-permute-start | bytes 1572872 | tf_op jit(solution)/shard_map/ppermute | solution.py:123
  786.4 149.3 %collective-permute-start.56 = (f32[128,1,1,1024]{3,0,2,1:T(8,128)}, f32[128,1,1,1024]{3,0,2,1:T(8,128)S(1)}, u32[]{:S(2)}, u32[]{:S(2)}) collective-permute-start(f32[128,1,1,1024]{3,0,2,1:T(8,128)} %get-tuple-element.51), channel_id=1, source_target_pairs={{0,4},{1,5},{2,6},{3,7},{4,0},{5,1},{6,2},{7,3},{8,12},{9,13},{10,... | collective-permute-start | bytes 1572872 | tf_op jit(solution)/shard_map/ppermute | solution.py:123
  792.6 263.0 %collective-permute-start.47 = (f32[256,2048]{1,0:T(8,128)}, f32[256,2048]{1,0:T(8,128)}, u32[]{:S(2)}, u32[]{:S(2)}) collective-permute-start(f32[256,2048]{1,0:T(8,128)} %get-tuple-element.18), channel_id=1, source_target_pairs={{0,1},{1,0},{2,3},{3,2},{4,5},{5,4},{6,7},{7,6},{8,9},{9,8},{10,11... | collective-permute-start | bytes 6291464 | tf_op jit(solution)/shard_map/ppermute | solution.py:123
  932.2 45.8 %collective-permute-start.58 = (f32[128,1,1,1024]{3,0,2,1:T(8,128)}, f32[128,1,1,1024]{3,0,2,1:T(8,128)}, u32[]{:S(2)}, u32[]{:S(2)}) collective-permute-start(f32[128,1,1,1024]{3,0,2,1:T(8,128)} %get-tuple-element.48), channel_id=1, source_target_pairs={{0,2},{1,3},{2,0},{3,1},{4,6},{5,7},{6,4},{7,5},{8,10},{9,11},{10,... | collective-permute-start | bytes 1572872 | tf_op jit(solution)/shard_map/ppermute | solution.py:123
  933.7 45.5 %collective-permute-start.59 = (f32[128,1,1,1024]{3,0,2,1:T(8,128)}, f32[128,1,1,1024]{3,0,2,1:T(8,128)}, u32[]{:S(2)}, u32[]{:S(2)}) collective-permute-start(f32[128,1,1,1024]{3,0,2,1:T(8,128)} %get-tuple-element.47), channel_id=1, source_target_pairs={{0,4},{1,5},{2,6},{3,7},{4,0},{5,1},{6,2},{7,3},{8,12},{9,13},{10,... | collective-permute-start | bytes 1572872 | tf_op jit(solution)/shard_map/ppermute | solution.py:123
  935.2 45.3 %collective-permute-start.60 = (f32[128,1,1,1024]{3,0,2,1:T(8,128)}, f32[128,1,1,1024]{3,0,2,1:T(8,128)}, u32[]{:S(2)}, u32[]{:S(2)}) collective-permute-start(f32[128,1,1,1024]{3,0,2,1:T(8,128)} %get-tuple-element.46), channel_id=1, source_target_pairs={{0,6},{1,7},{2,4},{3,5},{4,2},{5,3},{6,0},{7,1},{8,14},{9,15},{10,... | collective-permute-start | bytes 1572872 | tf_op jit(solution)/shard_map/ppermute | solution.py:123
  935.7 33.6 %collective-permute-start.57 = (f32[128,1,1,1024]{3,0,2,1:T(8,128)}, f32[128,1,1,1024]{3,0,2,1:T(8,128)}, u32[]{:S(2)}, u32[]{:S(2)}) collective-permute-start(f32[128,1,1,1024]{3,0,2,1:T(8,128)} %get-tuple-element.50), channel_id=1, source_target_pairs={{0,6},{1,7},{2,4},{3,5},{4,2},{5,3},{6,0},{7,1},{8,14},{9,15},{10,... | collective-permute-start | bytes 1572872 | tf_op jit(solution)/shard_map/ppermute | solution.py:123
  (122 other events, 2034.8 us)
Sparse Core Ops, SparseCore 0:
  594.0 41.6 reduce-scatter.6
  638.0 143.7 reduce-scatter.8
  784.2 145.2 reduce-scatter.10
  931.6 111.3 reduce-scatter.4
